TPU v7x, 32 devices: a whole 2x2x4 slice. The times are simulated.
32 devices in a mesh: seq: 8 (over z, core), fsdp: 4 (over y, x).
Axes of the slice: x: 2, y: 2, z: 4, core: 2. Of those that a mesh axis runs over, the one named last changes fastest.
Arguments:
- layer_inputs: bfloat16 [4, 1024, 4096], P('fsdp', 'seq'), may hold values from -8 to 8
- queries: bfloat16 [4, 1024, 4096], P('fsdp', 'seq'), may hold values from -6 to 6
- key_states: bfloat16 [4, 1024, 512], P('fsdp', 'seq'), may hold values from -4 to 4
- value_states: bfloat16 [4, 1024, 512], P('fsdp', 'seq'), may hold values from -1.75 to 1.75
- output_gradient: bfloat16 [4, 1024, 4096], P('fsdp', 'seq'), may hold values from -1.75 to 1.75
- doc_blocks: int32 [4, 4], P('fsdp'), may hold values from 1 to 3, 8 in all within a row
Outputs:
- query_grad: bfloat16 [4, 1024, 4096], P('fsdp', 'seq')
- key_grad: bfloat16 [4, 1024, 512], P('fsdp', 'seq')
- value_grad: bfloat16 [4, 1024, 512], P('fsdp', 'seq')
- value_weight_grad: bfloat16 [4096, 512], P('fsdp')
Inputs may be any that keep to these rules, and one draw needn't show every extreme that they name: `doc_blocks`: the lengths of each packed row sum to 8, and each row has a document of exactly 3 blocks.
All inputs are finite; a program needn't handle non-finite values.
Results may differ from a plain program's by a relative error of at most 0.017.
Values may be sent and summed in bfloat16 or wider, within the bound.
A program may use at most 64 MiB of HBM per device.

v0:
```python
import math
import jax
import jax.numpy as jnp
from jax import lax
from jax.sharding import PartitionSpec as P

KEY_VALUE_HEADS = 4
HEAD_SIZE = 128
BLOCK = 128
QUERY_PER_KEY = 8
BACK = 2
KEYS = 384


def passed_along(x, axis, by):
    peers = lax.axis_size(axis)
    pairs = [(i, i + by) for i in range(peers) if 0 <= i + by < peers]
    return lax.ppermute(x, axis, pairs)


def document_ids(positions, doc_ends):
    block_ids = jnp.floor_divide(positions, BLOCK)
    return jnp.sum((block_ids[:, None] >= doc_ends[None, :]).astype(jnp.int32), axis=1)


def group_grads(q_group, g_group, k_group, v_group, visible, softmax_factor_scale):
    scores = (
        jnp.einsum("rhd,kd->hrk", q_group, k_group, preferred_element_type=jnp.float32)
        * softmax_factor_scale
    )
    scores = jnp.where(visible[None], scores, -jnp.inf)
    row_max = jnp.max(scores, axis=-1, keepdims=True)
    exps = jnp.exp(scores - row_max)
    probs = exps / jnp.sum(exps, axis=-1, keepdims=True)
    d_probs = jnp.einsum("rhd,kd->hrk", g_group, v_group, preferred_element_type=jnp.float32)
    deltas = jnp.sum(probs * d_probs, axis=-1, keepdims=True)
    score_gradient = (probs * (d_probs - deltas)).astype(jnp.bfloat16)
    probability_reduced = probs.astype(jnp.bfloat16)
    value_portion = jnp.einsum(
        "hrk,rhd->kd", probability_reduced, g_group, preferred_element_type=jnp.float32
    )
    key_portion = (
        jnp.einsum("hrk,rhd->kd", score_gradient, q_group, preferred_element_type=jnp.float32)
        * softmax_factor_scale
    )
    query_portion = (
        jnp.einsum("hrk,kd->rhd", score_gradient, k_group, preferred_element_type=jnp.float32)
        * softmax_factor_scale
    )
    return (query_portion, key_portion, value_portion)


def shards(layer_inputs, queries, key_states, value_states, output_gradient, doc_blocks):
    token_rows = queries.shape[1]
    my_index = lax.axis_index("seq")
    own_keys = key_states[0]
    own_values = value_states[0]
    pad_rows = BACK * token_rows
    key_blocks = []
    value_blocks = []
    for distance in range(BACK, 0, -1):
        got_keys, got_values = passed_along((own_keys, own_values), "seq", distance)
        key_blocks.append(got_keys)
        value_blocks.append(got_values)
    key_blocks.append(own_keys)
    value_blocks.append(own_values)
    window_keys = jnp.concatenate(key_blocks, axis=0)
    window_values = jnp.concatenate(value_blocks, axis=0)
    doc_ends = jnp.cumsum(doc_blocks[0])
    first_query = my_index * token_rows
    q_pos = first_query + jnp.arange(token_rows, dtype=jnp.int32)
    k_pos = first_query - pad_rows + jnp.arange(KEYS, dtype=jnp.int32)
    same_doc = document_ids(k_pos, doc_ends)[None, :] == document_ids(q_pos, doc_ends)[:, None]
    visible = same_doc & (k_pos[None, :] >= 0) & (k_pos[None, :] <= q_pos[:, None])
    softmax_factor_scale = 1.0 / math.sqrt(HEAD_SIZE)
    query_head_states = queries[0].reshape(token_rows, KEY_VALUE_HEADS, QUERY_PER_KEY, HEAD_SIZE)
    gradient_heads = output_gradient[0].reshape(
        token_rows, KEY_VALUE_HEADS, QUERY_PER_KEY, HEAD_SIZE
    )
    query_portions = []
    key_parts = []
    value_parts = []
    for key_value_group in range(KEY_VALUE_HEADS):
        k_group = window_keys[:, key_value_group * HEAD_SIZE : (key_value_group + 1) * HEAD_SIZE]
        v_group = window_values[:, key_value_group * HEAD_SIZE : (key_value_group + 1) * HEAD_SIZE]
        query_portion, key_portion, value_portion = group_grads(
            query_head_states[:, key_value_group],
            gradient_heads[:, key_value_group],
            k_group,
            v_group,
            visible,
            softmax_factor_scale,
        )
        query_portions.append(query_portion)
        key_parts.append(key_portion)
        value_parts.append(value_portion)
    query_grad = (
        jnp.stack(query_portions, axis=1)
        .reshape(token_rows, KEY_VALUE_HEADS * QUERY_PER_KEY * HEAD_SIZE)
        .astype(jnp.bfloat16)
    )
    key_window = jnp.concatenate(key_parts, axis=1)
    value_window = jnp.concatenate(value_parts, axis=1)
    key_total = key_window[pad_rows:]
    value_total = value_window[pad_rows:]
    for distance in range(1, BACK + 1):
        lower = (BACK - distance) * token_rows
        got_keys, got_values = (
            passed_along(
                key_window[lower : lower + token_rows].astype(jnp.bfloat16), "seq", -distance
            ).astype(jnp.float32),
            passed_along(
                value_window[lower : lower + token_rows].astype(jnp.bfloat16), "seq", -distance
            ).astype(jnp.float32),
        )
        key_total = key_total + got_keys
        value_total = value_total + got_values
    key_grad = key_total.astype(jnp.bfloat16)
    value_grad = value_total.astype(jnp.bfloat16)
    local_inputs = layer_inputs[0]
    weight_share = lax.psum_scatter(
        lax.dot_general(
            local_inputs, value_grad, (((0,), (0,)), ((), ())), preferred_element_type=jnp.float32
        ).astype(jnp.bfloat16),
        "fsdp",
        scatter_dimension=0,
        tiled=True,
    )
    weight_total = lax.psum(weight_share, "seq").astype(jnp.float32)
    token_count = lax.axis_size("fsdp") * lax.axis_size("seq") * token_rows
    value_weight_grad = (weight_total / math.sqrt(token_count)).astype(jnp.bfloat16)
    return (query_grad[None], key_grad[None], value_grad[None], value_weight_grad)


def solution(mesh):
    placed = (
        P("fsdp", "seq", None),
        P("fsdp", "seq", None),
        P("fsdp", "seq", None),
        P("fsdp", "seq", None),
        P("fsdp", "seq", None),
        P("fsdp", None),
    )
    return jax.shard_map(
        shards,
        mesh=mesh,
        in_specs=placed,
        out_specs=(
            P("fsdp", "seq", None),
            P("fsdp", "seq", None),
            P("fsdp", "seq", None),
            P("fsdp", None),
        ),
        check_vma=False,
    )
```

profile of v0, /device:TPU:0, one launch (start us, length us, event | category | flops | bytes accessed | tf_op | source)
XLA Modules:
  0.0 170.2 jit_solution(6440243550890889599)
XLA Ops:
  7.2 2.5 %collective-permute-start.1 = (bf16[128,512]{1,0:T(8,128)(2,1)}, bf16[128,512]{1,0:T(8,128)(2,1)S(1)}, u32[]{:S(2)}, u32[]{:S(2)}) collective-permute-start(bf16[128,512]{1,0:T(8,128)(2,1)} %bitcast.294), channel_id=1, source_target_pairs={{0,4},{4,8},{8,12},{12,16},{16,20},{20,24},{24,28},{1,5},{5,9},{9,... | collective-permute-start | bytes 393224 | tf_op jit(solution)/shard_map/ppermute | solution.py:18
  9.8 4.5 %collective-permute-start = (bf16[128,512]{1,0:T(8,128)(2,1)}, bf16[128,512]{1,0:T(8,128)(2,1)S(1)}, u32[]{:S(2)}, u32[]{:S(2)}) collective-permute-start(bf16[128,512]{1,0:T(8,128)(2,1)} %bitcast.295), channel_id=1, source_target_pairs={{0,8},{4,12},{8,16},{12,20},{16,24},{20,28},{1,9},{5,13},{9,17},{1... | collective-permute-start | bytes 393224 | tf_op jit(solution)/shard_map/ppermute | solution.py:18
  15.9 1.6 copy.76
  17.5 1.3 copy.78
  19.8 1.8 %fusion.72 = (f32[8,128]{1,0:T(8,128)S(1)}, f32[8,128,384]{1,2,0:T(8,128)}) fusion(pred[128,384]{0,1:T(8,128)(4,1)S(1)} %compare_and_fusion, bf16[128,4,8,128]{0,3,2,1:T(8,128)(2,1)S(1)} %bitcast.276, bf16[384,512]{1,0:T(8,128)(2,1)S(1)} %pad_maximum_fusion.3), kind=kOutput, calls=%fused_computation.139 | convolution fusion | flops 102236544 | bytes 1986560 | tf_op jit(solution)/shard_map/sub | solution.py:33
  21.6 1.8 %fusion.73 = (f32[8,128]{1,0:T(8,128)S(1)}, f32[8,128,384]{1,2,0:T(8,128)}) fusion(pred[128,384]{0,1:T(8,128)(4,1)S(1)} %compare_and_fusion, bf16[128,4,8,128]{0,3,2,1:T(8,128)(2,1)S(1)} %bitcast.277, bf16[384,512]{1,0:T(8,128)(2,1)S(1)} %pad_maximum_fusion.3), kind=kOutput, calls=%fused_computation.140 | convolution fusion | flops 102236544 | bytes 1986560 | tf_op jit(solution)/shard_map/sub | solution.py:33
  23.4 1.8 %fusion.74 = (f32[8,128]{1,0:T(8,128)S(1)}, f32[8,128,384]{1,2,0:T(8,128)}) fusion(pred[128,384]{0,1:T(8,128)(4,1)S(1)} %compare_and_fusion, bf16[128,4,8,128]{0,3,2,1:T(8,128)(2,1)S(1)} %bitcast.278, bf16[384,512]{1,0:T(8,128)(2,1)S(1)} %pad_maximum_fusion.3), kind=kOutput, calls=%fused_computation.141 | convolution fusion | flops 102236544 | bytes 1986560 | tf_op jit(solution)/shard_map/sub | solution.py:33
  25.1 1.8 %fusion.71 = (f32[8,128]{1,0:T(8,128)S(1)}, f32[8,128,384]{1,2,0:T(8,128)}) fusion(pred[128,384]{0,1:T(8,128)(4,1)S(1)} %compare_and_fusion, bf16[128,4,8,128]{0,3,2,1:T(8,128)(2,1)S(1)} %bitcast.279, bf16[384,512]{1,0:T(8,128)(2,1)S(1)} %pad_maximum_fusion.3), kind=kOutput, calls=%fused_computation.138 | convolution fusion | flops 102236544 | bytes 1986560 | tf_op jit(solution)/shard_map/sub | solution.py:33
  26.9 1.9 %convolution_bitcast_fusion.1 = f32[384,128]{0,1:T(8,128)S(1)} fusion(bf16[128,4,8,128]{0,3,2,1:T(8,128)(2,1)} %bitcast.286, f32[8,128,384]{1,2,0:T(8,128)} %get-tuple-element.25, f32[8,128]{1,0:T(8,128)S(1)} %get-tuple-element.24), kind=kOutput, calls=%fused_computation.52 | convolution fusion | flops 101449728 | bytes 2035712 | tf_op jit(solution)/shard_map/hrk,rhd->kd/dot_general | solution.py:39
  35.1 1.5 collective-permute-done.6
  36.6 6.5 %collective-permute-done.7 = bf16[128,512]{0,1:T(8,128)(2,1)S(1)} collective-permute-done((bf16[128,512]{0,1:T(8,128)(2,1)S(1)}, bf16[128,512]{0,1:T(8,128)(2,1)S(1)}, u32[]{:S(2)}, u32[]{:S(2)}) %collective-permute-start.7) | collective-permute-done | bytes 131104 | tf_op jit(solution)/shard_map/ppermute | solution.py:18
  43.2 3.2 %fusion.4 = bf16[4096,512]{0,1:T(8,128)(2,1)} fusion(bf16[128,512]{0,1:T(8,128)(2,1)S(1)} %fusion.43, bf16[1,128,4096]{2,1,0:T(8,128)(2,1)S(1)} %copy-done), kind=kOutput, calls=%fused_computation.5 | convolution fusion | flops 538968064 | bytes 5373952 | tf_op jit(solution)/shard_map/dot_general | solution.py:122
  47.3 1.5 collective-permute-start.3
  48.8 3.9 %collective-permute-start.2 = (bf16[128,512]{1,0:T(8,128)(2,1)S(1)}, bf16[128,512]{1,0:T(8,128)(2,1)S(1)}, u32[]{:S(2)}, u32[]{:S(2)}) collective-permute-start(bf16[128,512]{1,0:T(8,128)(2,1)S(1)} %bitcast.298), channel_id=1, source_target_pairs={{0,8},{4,12},{8,16},{12,20},{16,24},{20,28},{1,9},{5,13},{9,17},{1... | collective-permute-start | bytes 393224 | tf_op jit(solution)/shard_map/ppermute | solution.py:18
  52.7 3.6 %collective-permute-done.2 = bf16[128,512]{1,0:T(8,128)(2,1)S(1)} collective-permute-done((bf16[128,512]{1,0:T(8,128)(2,1)S(1)}, bf16[128,512]{1,0:T(8,128)(2,1)S(1)}, u32[]{:S(2)}, u32[]{:S(2)}) %collective-permute-start.2) | collective-permute-done | bytes 131104 | tf_op jit(solution)/shard_map/ppermute | solution.py:18
  56.3 1.4 fusion.12
  65.4 2.3 %copy.110 = bf16[1,128,4096]{2,1,0:T(8,128)(2,1)} copy(bf16[1,128,4096]{1,2,0:T(8,128)(2,1)} %bitcast.284) | data formatting | bytes 2097152
  67.7 1.5 fusion.34
  69.2 1.4 fusion.35
  71.4 27.5 %reduce-scatter.2.cloned.1.call-done = bf16[1024,512]{0,1:T(8,128)(2,1)} async-done(((bf16[4096,512]{0,1:T(8,128)(2,1)}), bf16[1024,512]{0,1:T(8,128)(2,1)}) %reduce-scatter.2.cloned.1.call-update) | async-done | bytes 1048592 | tf_op jit(solution)/shard_map/reduce_scatter | solution.py:121
  102.5 6.2 %collective-permute-done.5 = bf16[128,512]{0,1:T(8,128)(2,1)S(1)} collective-permute-done((bf16[128,512]{0,1:T(8,128)(2,1)S(1)}, bf16[128,512]{0,1:T(8,128)(2,1)S(1)}, u32[]{:S(2)}, u32[]{:S(2)}) %collective-permute-start.5) | collective-permute-done | bytes 131104 | tf_op jit(solution)/shard_map/ppermute | solution.py:18
  109.4 51.2 %all-reduce.2.cloned.1.call-done = bf16[1024,512]{0,1:T(8,128)(2,1)} async-done(((bf16[1024,512]{0,1:T(8,128)(2,1)}), bf16[1024,512]{0,1:T(8,128)(2,1)}) %all-reduce.2.cloned.1.call-update) | async-done | bytes 1048592 | tf_op jit(solution)/shard_map/psum | solution.py:129
  160.6 1.4 multiply_convert_fusion
  162.0 1.3 copy.113
  (94 shorter events, 22.2 us)
Async XLA Ops:
  7.2 36.0 %copy-start = (bf16[1,128,4096]{2,1,0:T(8,128)(2,1)S(1)}, bf16[1,128,4096]{2,1,0:T(8,128)(2,1)}, u32[]{:S(2)}) copy-start(bf16[1,128,4096]{2,1,0:T(8,128)(2,1)} %param.6) | copy-start | bytes 3145732
  7.2 10.3 %copy-start.17 = (bf16[1,128,4096]{2,1,0:T(8,128)(2,1)S(1)}, bf16[1,128,4096]{2,1,0:T(8,128)(2,1)}, u32[]{:S(2)}) copy-start(bf16[1,128,4096]{2,1,0:T(8,128)(2,1)} %param.10) | copy-start | bytes 3145732
  7.2 91.8 %reduce-scatter.2.cloned.1.call-start = ((), (), s32[]{:S(2)}) async-start(), calls=%async_computation.1 | async-start | bytes 5242880 | tf_op jit(solution)/shard_map/reduce_scatter | solution.py:121
  7.2 12.5 %collective-permute-start.1 = (bf16[128,512]{1,0:T(8,128)(2,1)}, bf16[128,512]{1,0:T(8,128)(2,1)S(1)}, u32[]{:S(2)}, u32[]{:S(2)}) collective-permute-start(bf16[128,512]{1,0:T(8,128)(2,1)} %bitcast.294), channel_id=1, source_target_pairs={{0,4},{4,8},{8,12},{12,16},{16,20},{20,24},{24,28},{1,5},{5,9},{9,... | collective-permute-start | bytes 393224 | tf_op jit(solution)/shard_map/ppermute | solution.py:18
  9.8 9.9 %collective-permute-start = (bf16[128,512]{1,0:T(8,128)(2,1)}, bf16[128,512]{1,0:T(8,128)(2,1)S(1)}, u32[]{:S(2)}, u32[]{:S(2)}) collective-permute-start(bf16[128,512]{1,0:T(8,128)(2,1)} %bitcast.295), channel_id=1, source_target_pairs={{0,8},{4,12},{8,16},{12,20},{16,24},{20,28},{1,9},{5,13},{9,17},{1... | collective-permute-start | bytes 393224 | tf_op jit(solution)/shard_map/ppermute | solution.py:18
  17.5 7.7 %copy-start.3 = (bf16[1,128,4096]{1,2,0:T(8,128)(2,1)}, bf16[1,128,4096]{1,2,0:T(8,128)(2,1)S(1)}, u32[]{:S(2)}) copy-start(bf16[1,128,4096]{1,2,0:T(8,128)(2,1)S(1)} %copy.76) | copy-start | bytes 3145732
  17.5 2.2 %copy-start.20 = (bf16[1,128,512]{2,1,0:T(8,128)(2,1)S(1)}, bf16[1,128,512]{2,1,0:T(8,128)(2,1)}, u32[]{:S(2)}) copy-start(bf16[1,128,512]{2,1,0:T(8,128)(2,1)} %param.8) | copy-start | bytes 393220
  19.8 40.3 %copy-start.7 = (bf16[384,512]{1,0:T(8,128)(2,1)}, bf16[384,512]{1,0:T(8,128)(2,1)S(1)}, u32[]{:S(2)}) copy-start(bf16[384,512]{1,0:T(8,128)(2,1)S(1)} %pad_maximum_fusion.3) | copy-start | bytes 1179652
  26.9 2.0 %copy-start.13 = (f32[8,128,384]{1,2,0:T(8,128)S(1)}, f32[8,128,384]{1,2,0:T(8,128)}, u32[]{:S(2)}) copy-start(f32[8,128,384]{1,2,0:T(8,128)} %get-tuple-element.29) | copy-start | bytes 4718596
  26.9 2.2 %copy-start.18 = (bf16[1,128,4096]{1,2,0:T(8,128)(2,1)S(1)}, bf16[1,128,4096]{1,2,0:T(8,128)(2,1)}, u32[]{:S(2)}) copy-start(bf16[1,128,4096]{1,2,0:T(8,128)(2,1)} %copy.78) | copy-start | bytes 3145732
  32.5 4.1 %collective-permute-start.6 = (bf16[128,512]{0,1:T(8,128)(2,1)S(1)}, bf16[128,512]{0,1:T(8,128)(2,1)S(1)}, u32[]{:S(2)}, u32[]{:S(2)}) collective-permute-start(bf16[128,512]{0,1:T(8,128)(2,1)S(1)} %get-tuple-element.16), channel_id=1, source_target_pairs={{4,0},{8,4},{12,8},{16,12},{20,16},{24,20},{28,24},{5,1},{9,5},{13... | collective-permute-start | bytes 393224 | tf_op jit(solution)/shard_map/ppermute | solution.py:18
  33.8 9.4 %collective-permute-start.7 = (bf16[128,512]{0,1:T(8,128)(2,1)S(1)}, bf16[128,512]{0,1:T(8,128)(2,1)S(1)}, u32[]{:S(2)}, u32[]{:S(2)}) collective-permute-start(bf16[128,512]{0,1:T(8,128)(2,1)S(1)} %get-tuple-element.17), channel_id=1, source_target_pairs={{8,0},{12,4},{16,8},{20,12},{24,16},{28,20},{9,1},{13,5},{17,9},{2... | collective-permute-start | bytes 393224 | tf_op jit(solution)/shard_map/ppermute | solution.py:18
  46.4 9.9 %copy-start.15 = (f32[8,128,384]{1,2,0:T(8,128)S(1)}, f32[8,128,384]{1,2,0:T(8,128)}, u32[]{:S(2)}) copy-start(f32[8,128,384]{1,2,0:T(8,128)} %get-tuple-element.25) | copy-start | bytes 4718596
  46.4 114.2 %all-reduce.2.cloned.1.call-start = ((), (), s32[]{:S(2)}) async-start(), calls=%async_computation.2 | async-start | bytes 2097152 | tf_op jit(solution)/shard_map/psum | solution.py:129
  47.3 5.4 %collective-permute-start.3 = (bf16[128,512]{1,0:T(8,128)(2,1)S(1)}, bf16[128,512]{1,0:T(8,128)(2,1)S(1)}, u32[]{:S(2)}, u32[]{:S(2)}) collective-permute-start(bf16[128,512]{1,0:T(8,128)(2,1)S(1)} %bitcast.297), channel_id=1, source_target_pairs={{0,4},{4,8},{8,12},{12,16},{16,20},{20,24},{24,28},{1,5},{5,9},{9,... | collective-permute-start | bytes 393224 | tf_op jit(solution)/shard_map/ppermute | solution.py:18
  48.8 7.5 %collective-permute-start.2 = (bf16[128,512]{1,0:T(8,128)(2,1)S(1)}, bf16[128,512]{1,0:T(8,128)(2,1)S(1)}, u32[]{:S(2)}, u32[]{:S(2)}) collective-permute-start(bf16[128,512]{1,0:T(8,128)(2,1)S(1)} %bitcast.298), channel_id=1, source_target_pairs={{0,8},{4,12},{8,16},{12,20},{16,24},{20,28},{1,9},{5,13},{9,17},{1... | collective-permute-start | bytes 393224 | tf_op jit(solution)/shard_map/ppermute | solution.py:18
  57.8 1.7 copy-start.19
  61.6 1.7 %copy-start.10 = (f32[8,128,384]{1,2,0:T(8,128)S(1)}, f32[8,128,384]{1,2,0:T(8,128)}, u32[]{:S(2)}) copy-start(f32[8,128,384]{1,2,0:T(8,128)} %get-tuple-element.33) | copy-start | bytes 4718596
  67.7 2.9 %copy-start.2 = (bf16[8,128,384]{1,2,0:T(8,128)(2,1)S(1)}, bf16[8,128,384]{1,2,0:T(8,128)(2,1)}, u32[]{:S(2)}) copy-start(bf16[8,128,384]{1,2,0:T(8,128)(2,1)} %copy-done.1) | copy-start | bytes 2359300
  67.7 2.9 %copy-start.4 = (bf16[1,128,4096]{1,2,0:T(8,128)(2,1)S(1)}, bf16[1,128,4096]{1,2,0:T(8,128)(2,1)}, u32[]{:S(2)}) copy-start(bf16[1,128,4096]{1,2,0:T(8,128)(2,1)} %copy-done.3) | copy-start | bytes 3145732
  69.2 2.2 %copy-start.5 = (f32[384,128]{0,1:T(8,128)}, f32[384,128]{0,1:T(8,128)S(1)}, u32[]{:S(2)}) copy-start(f32[384,128]{0,1:T(8,128)S(1)} %fusion.34) | copy-start | bytes 589828
  71.4 30.2 %copy-start.6 = (f32[384,128]{0,1:T(8,128)S(1)}, f32[384,128]{0,1:T(8,128)}, u32[]{:S(2)}) copy-start(f32[384,128]{0,1:T(8,128)} %copy-done.5) | copy-start | bytes 589828
  99.0 3.4 %collective-permute-start.4 = (bf16[128,512]{0,1:T(8,128)(2,1)S(1)}, bf16[128,512]{0,1:T(8,128)(2,1)S(1)}, u32[]{:S(2)}, u32[]{:S(2)}) collective-permute-start(bf16[128,512]{0,1:T(8,128)(2,1)S(1)} %get-tuple-element.18), channel_id=1, source_target_pairs={{4,0},{8,4},{12,8},{16,12},{20,16},{24,20},{28,24},{5,1},{9,5},{13... | collective-permute-start | bytes 393224 | tf_op jit(solution)/shard_map/ppermute | solution.py:18
  100.3 8.3 %collective-permute-start.5 = (bf16[128,512]{0,1:T(8,128)(2,1)S(1)}, bf16[128,512]{0,1:T(8,128)(2,1)S(1)}, u32[]{:S(2)}, u32[]{:S(2)}) collective-permute-start(bf16[128,512]{0,1:T(8,128)(2,1)S(1)} %get-tuple-element.19), channel_id=1, source_target_pairs={{8,0},{12,4},{16,8},{20,12},{24,16},{28,20},{9,1},{13,5},{17,9},{2... | collective-permute-start | bytes 393224 | tf_op jit(solution)/shard_map/ppermute | solution.py:18
  (8 other events, 10.5 us)
Sparse Core Ops, SparseCore 0:
  46.5 52.3 reduce-scatter.1
  101.3 59.2 all-reduce.1
where the time goes:
time: 171 us; the launch traced here: 170 us
  waiting for transfers between devices  96.5 us (56%)
  matrix products  20.8 us (12%)
  starting transfers between devices  17.7 us (10%)
  between operations  14.6 us (9%)
  local copies, waits for them, and re-layouts  14.5 us (8%)
  other arithmetic  6.15 us (4%)
    psum x1, waiting for transfers between devices, shards(): weight_total = lax.psum(weight_share, 'seq').astype(jnp.float32)  51.2 us
    reduce_scatter x1, waiting for transfers between devices, shards(): lax.psum_scatter(lax.dot_general(local_inputs, value_grad, (((0,), (0,)),...  27.5 us
    ppermute x8, waiting for transfers between devices, passed_along(): return lax.ppermute(x, axis, pairs)  17.8 us
    ppermute x8, starting transfers between devices, passed_along(): return lax.ppermute(x, axis, pairs)  17.6 us
    unnamed x50, local copies, waits for them, and re-layouts  14.5 us
    sub x4, matrix products, group_grads(): exps = jnp.exp(scores - row_max)  7.15 us
    dot_general x4, matrix products, group_grads(): jnp.einsum('hrk,rhd->kd', score_gradient, q_group, preferred_element_type...  3.6 us
  transfers between devices with their start and end apart: 10, of which 6 were waited for; matrix products, arithmetic and copies ran while one was open for 11% of the time, Pallas kernels for 0%

commit v1 on v0

--- a/solution.py
+++ b/solution.py
@@ -1,3 +1,4 @@
+import functools
 import math
 import jax
 import jax.numpy as jnp
@@ -10,6 +11,15 @@
 QUERY_PER_KEY = 8
 BACK = 2
 KEYS = 384
+
+
+def write_the_meshes(packet, link_axis):
+    b_now = lax.all_gather(packet, link_axis)
+    new = jnp.sum(b_now, axis=0)
+    return new
+
+
+pipes_balance = functools.partial(write_the_meshes, link_axis="seq")
 
 
 def passed_along(x, axis, by):
@@ -126,7 +136,7 @@
         scatter_dimension=0,
         tiled=True,
     )
-    weight_total = lax.psum(weight_share, "seq").astype(jnp.float32)
+    weight_total = pipes_balance(weight_share).astype(jnp.float32)
     token_count = lax.axis_size("fsdp") * lax.axis_size("seq") * token_rows
     value_weight_grad = (weight_total / math.sqrt(token_count)).astype(jnp.bfloat16)
     return (query_grad[None], key_grad[None], value_grad[None], value_weight_grad)

time: 171 us -> 223 us (1.30)
  waiting for transfers between devices: 96.5 us -> 123 us
  local copies, waits for them, and re-layouts: 14.5 us -> 30.6 us
  other arithmetic: 6.15 us -> 15.8 us
    psum x1 -> x0, waiting for transfers between devices: 51.2 us -> none  [shards(): weight_total = lax.psum(weight_share, 'seq').astype(jnp.float32)]
    all_gather x0 -> x1, waiting for transfers between devices: none -> 40.1 us  [write_the_meshes(): b_now = lax.all_gather(packet, link_axis)]
    reduce_scatter x1, waiting for transfers between devices: 27.5 us -> 52.5 us  [shards(): lax.psum_scatter(lax.dot_general(local_inputs, value_grad, (((0,), (0,)),...]
    unnamed x50 -> x47, local copies, waits for them, and re-layouts: 14.5 us -> 30.5 us
    ppermute x8, waiting for transfers between devices: 17.8 us -> 30.2 us  [passed_along(): return lax.ppermute(x, axis, pairs)]
    reduce_sum x0 -> x1, other arithmetic: none -> 10.9 us  [write_the_meshes(): new = jnp.sum(b_now, axis=0)]
  transfers between devices with their start and end apart: 10 -> 10, of which waited for: 6 -> 6; matrix products, arithmetic and copies ran while one was open for 11% -> 8% of each run, Pallas kernels for 0% -> 0%
where the time goes in v1:
time: 223 us; the launch traced here: 222 us
  waiting for transfers between devices  123 us (55%)
  local copies, waits for them, and re-layouts  30.6 us (14%)
  matrix products  20.7 us (9%)
  starting transfers between devices  17.8 us (8%)
  other arithmetic  15.8 us (7%)
  between operations  14.6 us (7%)
    reduce_scatter x1, waiting for transfers between devices, shards(): lax.psum_scatter(lax.dot_general(local_inputs, value_grad, (((0,), (0,)),...  52.5 us
    all_gather x1, waiting for transfers between devices, write_the_meshes(): b_now = lax.all_gather(packet, link_axis)  40.1 us
    unnamed x47, local copies, waits for them, and re-layouts  30.5 us
    ppermute x8, waiting for transfers between devices, passed_along(): return lax.ppermute(x, axis, pairs)  30.2 us
    ppermute x8, starting transfers between devices, passed_along(): return lax.ppermute(x, axis, pairs)  17.7 us
    reduce_sum x1, other arithmetic, write_the_meshes(): new = jnp.sum(b_now, axis=0)  10.9 us
    sub x4, matrix products, group_grads(): exps = jnp.exp(scores - row_max)  7.08 us
  transfers between devices with their start and end apart: 10, of which 6 were waited for; matrix products, arithmetic and copies ran while one was open for 8% of the time, Pallas kernels for 0%

profile of v1, /device:TPU:0, one launch (start us, length us, event | category | flops | bytes accessed | tf_op | source)
XLA Modules:
  0.0 222.2 jit_solution(8977055975731507136)
XLA Ops:
  7.2 2.5 %collective-permute-start.1 = (bf16[128,512]{1,0:T(8,128)(2,1)}, bf16[128,512]{1,0:T(8,128)(2,1)S(1)}, u32[]{:S(2)}, u32[]{:S(2)}) collective-permute-start(bf16[128,512]{1,0:T(8,128)(2,1)} %bitcast.300), channel_id=1, source_target_pairs={{0,4},{4,8},{8,12},{12,16},{16,20},{20,24},{24,28},{1,5},{5,9},{9,... | collective-permute-start | bytes 393224 | tf_op jit(solution)/shard_map/ppermute | solution.py:28
  9.8 4.5 %collective-permute-start = (bf16[128,512]{1,0:T(8,128)(2,1)}, bf16[128,512]{1,0:T(8,128)(2,1)S(1)}, u32[]{:S(2)}, u32[]{:S(2)}) collective-permute-start(bf16[128,512]{1,0:T(8,128)(2,1)} %bitcast.301), channel_id=1, source_target_pairs={{0,8},{4,12},{8,16},{12,20},{16,24},{20,28},{1,9},{5,13},{9,17},{1... | collective-permute-start | bytes 393224 | tf_op jit(solution)/shard_map/ppermute | solution.py:28
  15.9 1.6 copy.112
  19.8 1.7 fusion.72
  21.5 1.8 fusion.73
  23.3 1.8 fusion.74
  25.1 1.7 fusion.71
  26.9 1.9 convolution_bitcast_fusion.1
  35.0 1.5 collective-permute-done.6
  36.5 6.5 %collective-permute-done.7 = bf16[128,512]{0,1:T(8,128)(2,1)S(1)} collective-permute-done((bf16[128,512]{0,1:T(8,128)(2,1)S(1)}, bf16[128,512]{0,1:T(8,128)(2,1)S(1)}, u32[]{:S(2)}, u32[]{:S(2)}) %collective-permute-start.7) | collective-permute-done | bytes 131104 | tf_op jit(solution)/shard_map/ppermute | solution.py:28
  43.1 3.2 %fusion.4 = bf16[4096,512]{0,1:T(8,128)(2,1)} fusion(bf16[128,512]{0,1:T(8,128)(2,1)S(1)} %fusion.43, bf16[1,128,4096]{2,1,0:T(8,128)(2,1)S(1)} %copy-done), kind=kOutput, calls=%fused_computation.6 | convolution fusion | flops 538968064 | bytes 5373952 | tf_op jit(solution)/shard_map/dot_general | solution.py:132
  46.4 52.5 %reduce-scatter.2.cloned.1.call-done = bf16[1024,512]{0,1:T(8,128)(2,1)} async-done(((bf16[4096,512]{0,1:T(8,128)(2,1)}), bf16[1024,512]{0,1:T(8,128)(2,1)}) %reduce-scatter.2.cloned.1.call-update) | async-done | bytes 1048592 | tf_op jit(solution)/shard_map/reduce_scatter | solution.py:131
  98.9 1.6 collective-permute-start.3
  100.5 3.7 %collective-permute-start.2 = (bf16[128,512]{1,0:T(8,128)(2,1)S(1)}, bf16[128,512]{1,0:T(8,128)(2,1)S(1)}, u32[]{:S(2)}, u32[]{:S(2)}) collective-permute-start(bf16[128,512]{1,0:T(8,128)(2,1)S(1)} %bitcast.304), channel_id=1, source_target_pairs={{0,8},{4,12},{8,16},{12,20},{16,24},{20,28},{1,9},{5,13},{9,17},{1... | collective-permute-start | bytes 393224 | tf_op jit(solution)/shard_map/ppermute | solution.py:28
  104.2 3.2 %collective-permute-done.2 = bf16[128,512]{1,0:T(8,128)(2,1)S(1)} collective-permute-done((bf16[128,512]{1,0:T(8,128)(2,1)S(1)}, bf16[128,512]{1,0:T(8,128)(2,1)S(1)}, u32[]{:S(2)}, u32[]{:S(2)}) %collective-permute-start.2) | collective-permute-done | bytes 131104 | tf_op jit(solution)/shard_map/ppermute | solution.py:28
  107.5 1.5 fusion.12
  117.2 2.3 %copy.146 = bf16[1,128,4096]{2,1,0:T(8,128)(2,1)} copy(bf16[1,128,4096]{1,2,0:T(8,128)(2,1)} %bitcast.290) | data formatting | bytes 2097152
  119.5 1.5 fusion.34
  121.0 1.3 fusion.35
  124.5 1.5 collective-permute-start.5
  126.8 19.0 %collective-permute-done.5 = bf16[128,512]{0,1:T(8,128)(2,1)S(1)} collective-permute-done((bf16[128,512]{0,1:T(8,128)(2,1)S(1)}, bf16[128,512]{0,1:T(8,128)(2,1)S(1)}, u32[]{:S(2)}, u32[]{:S(2)}) %collective-permute-start.5) | collective-permute-done | bytes 131104 | tf_op jit(solution)/shard_map/ppermute | solution.py:28
  146.6 40.1 %all-gather.3.cloned.1.call-done = bf16[8192,512]{0,1:T(8,128)(2,1)} async-done(((bf16[1024,512]{0,1:T(8,128)(2,1)}), bf16[8192,512]{0,1:T(8,128)(2,1)}) %all-gather.3.cloned.1.call-update) | async-done | bytes 8388624 | tf_op jit(solution)/shard_map/all_gather | solution.py:17
  186.7 16.3 %copy.186 = bf16[64,8,8,1024]{3,2,1,0:T(8,128)(2,1)} copy(bf16[64,8,8,1024]{3,1,2,0:T(8,128)(2,1)} %bitcast.281) | data formatting | bytes 16777216
  203.0 10.9 %bitcast_reduce_fusion = bf16[1024,512]{0,1:T(8,128)(2,1)S(1)} fusion(bf16[64,8,8,1024]{3,2,1,0:T(8,128)(2,1)} %copy.186), kind=kLoop, calls=%fused_computation.4 | loop fusion | flops 3670016 | bytes 9437184 | tf_op jit(solution)/shard_map/reduce_sum | solution.py:18
  (92 shorter events, 23.6 us)
Async XLA Ops:
  7.2 36.0 %copy-start = (bf16[1,128,4096]{2,1,0:T(8,128)(2,1)S(1)}, bf16[1,128,4096]{2,1,0:T(8,128)(2,1)}, u32[]{:S(2)}) copy-start(bf16[1,128,4096]{2,1,0:T(8,128)(2,1)} %param.6) | copy-start | bytes 3145732
  7.2 10.3 %copy-start.15 = (bf16[1,128,4096]{2,1,0:T(8,128)(2,1)S(1)}, bf16[1,128,4096]{2,1,0:T(8,128)(2,1)}, u32[]{:S(2)}) copy-start(bf16[1,128,4096]{2,1,0:T(8,128)(2,1)} %param.10) | copy-start | bytes 3145732
  7.2 91.7 %reduce-scatter.2.cloned.1.call-start = ((), (), s32[]{:S(2)}) async-start(), calls=%async_computation.1 | async-start | bytes 5242880 | tf_op jit(solution)/shard_map/reduce_scatter | solution.py:131
  7.2 12.5 %collective-permute-start.1 = (bf16[128,512]{1,0:T(8,128)(2,1)}, bf16[128,512]{1,0:T(8,128)(2,1)S(1)}, u32[]{:S(2)}, u32[]{:S(2)}) collective-permute-start(bf16[128,512]{1,0:T(8,128)(2,1)} %bitcast.300), channel_id=1, source_target_pairs={{0,4},{4,8},{8,12},{12,16},{16,20},{20,24},{24,28},{1,5},{5,9},{9,... | collective-permute-start | bytes 393224 | tf_op jit(solution)/shard_map/ppermute | solution.py:28
  9.8 9.9 %collective-permute-start = (bf16[128,512]{1,0:T(8,128)(2,1)}, bf16[128,512]{1,0:T(8,128)(2,1)S(1)}, u32[]{:S(2)}, u32[]{:S(2)}) collective-permute-start(bf16[128,512]{1,0:T(8,128)(2,1)} %bitcast.301), channel_id=1, source_target_pairs={{0,8},{4,12},{8,16},{12,20},{16,24},{20,28},{1,9},{5,13},{9,17},{1... | collective-permute-start | bytes 393224 | tf_op jit(solution)/shard_map/ppermute | solution.py:28
  17.5 7.6 %copy-start.3 = (bf16[1,128,4096]{1,2,0:T(8,128)(2,1)}, bf16[1,128,4096]{1,2,0:T(8,128)(2,1)S(1)}, u32[]{:S(2)}) copy-start(bf16[1,128,4096]{1,2,0:T(8,128)(2,1)S(1)} %copy.112) | copy-start | bytes 3145732
  17.5 2.2 copy-start.18
  19.8 92.4 %copy-start.5 = (bf16[384,512]{1,0:T(8,128)(2,1)}, bf16[384,512]{1,0:T(8,128)(2,1)S(1)}, u32[]{:S(2)}) copy-start(bf16[384,512]{1,0:T(8,128)(2,1)S(1)} %pad_maximum_fusion.3) | copy-start | bytes 1179652
  26.9 2.0 copy-start.11
  26.9 2.2 %copy-start.16 = (bf16[1,128,4096]{1,2,0:T(8,128)(2,1)S(1)}, bf16[1,128,4096]{1,2,0:T(8,128)(2,1)}, u32[]{:S(2)}) copy-start(bf16[1,128,4096]{1,2,0:T(8,128)(2,1)} %copy.114) | copy-start | bytes 3145732
  32.4 4.1 %collective-permute-start.6 = (bf16[128,512]{0,1:T(8,128)(2,1)S(1)}, bf16[128,512]{0,1:T(8,128)(2,1)S(1)}, u32[]{:S(2)}, u32[]{:S(2)}) collective-permute-start(bf16[128,512]{0,1:T(8,128)(2,1)S(1)} %get-tuple-element.20), channel_id=1, source_target_pairs={{4,0},{8,4},{12,8},{16,12},{20,16},{24,20},{28,24},{5,1},{9,5},{13... | collective-permute-start | bytes 393224 | tf_op jit(solution)/shard_map/ppermute | solution.py:28
  33.7 9.4 %collective-permute-start.7 = (bf16[128,512]{0,1:T(8,128)(2,1)S(1)}, bf16[128,512]{0,1:T(8,128)(2,1)S(1)}, u32[]{:S(2)}, u32[]{:S(2)}) collective-permute-start(bf16[128,512]{0,1:T(8,128)(2,1)S(1)} %get-tuple-element.21), channel_id=1, source_target_pairs={{8,0},{12,4},{16,8},{20,12},{24,16},{28,20},{9,1},{13,5},{17,9},{2... | collective-permute-start | bytes 393224 | tf_op jit(solution)/shard_map/ppermute | solution.py:28
  46.3 52.6 %copy-start.19 = (bf16[1,128,512]{2,1,0:T(8,128)(2,1)S(1)}, bf16[1,128,512]{2,1,0:T(8,128)(2,1)}, u32[]{:S(2)}) copy-start(bf16[1,128,512]{2,1,0:T(8,128)(2,1)} %param.9) | copy-start | bytes 393220
  46.3 61.2 %copy-start.13 = (f32[8,128,384]{1,2,0:T(8,128)S(1)}, f32[8,128,384]{1,2,0:T(8,128)}, u32[]{:S(2)}) copy-start(f32[8,128,384]{1,2,0:T(8,128)} %get-tuple-element.29) | copy-start | bytes 4718596
  46.3 140.3 %all-gather.3.cloned.1.call-start = ((), (), s32[]{:S(2)}) async-start(), calls=%async_computation.2 | async-start | bytes 9437184 | tf_op jit(solution)/shard_map/all_gather | solution.py:17
  98.9 5.3 %collective-permute-start.3 = (bf16[128,512]{1,0:T(8,128)(2,1)S(1)}, bf16[128,512]{1,0:T(8,128)(2,1)S(1)}, u32[]{:S(2)}, u32[]{:S(2)}) collective-permute-start(bf16[128,512]{1,0:T(8,128)(2,1)S(1)} %bitcast.303), channel_id=1, source_target_pairs={{0,4},{4,8},{8,12},{12,16},{16,20},{20,24},{24,28},{1,5},{5,9},{9,... | collective-permute-start | bytes 393224 | tf_op jit(solution)/shard_map/ppermute | solution.py:28
  100.5 7.0 %collective-permute-start.2 = (bf16[128,512]{1,0:T(8,128)(2,1)S(1)}, bf16[128,512]{1,0:T(8,128)(2,1)S(1)}, u32[]{:S(2)}, u32[]{:S(2)}) collective-permute-start(bf16[128,512]{1,0:T(8,128)(2,1)S(1)} %bitcast.304), channel_id=1, source_target_pairs={{0,8},{4,12},{8,16},{12,20},{16,24},{20,28},{1,9},{5,13},{9,17},{1... | collective-permute-start | bytes 393224 | tf_op jit(solution)/shard_map/ppermute | solution.py:28
  107.5 1.7 copy-start.14
  109.2 1.9 copy-start.12
  109.2 2.3 %copy-start.17 = (bf16[1,128,4096]{1,2,0:T(8,128)(2,1)S(1)}, bf16[1,128,4096]{1,2,0:T(8,128)(2,1)}, u32[]{:S(2)}) copy-start(bf16[1,128,4096]{1,2,0:T(8,128)(2,1)} %copy.114) | copy-start | bytes 3145732
  119.5 2.8 %copy-start.2 = (bf16[8,128,384]{1,2,0:T(8,128)(2,1)S(1)}, bf16[8,128,384]{1,2,0:T(8,128)(2,1)}, u32[]{:S(2)}) copy-start(bf16[8,128,384]{1,2,0:T(8,128)(2,1)} %copy-done.1) | copy-start | bytes 2359300
  119.5 2.8 %copy-start.4 = (bf16[1,128,4096]{1,2,0:T(8,128)(2,1)S(1)}, bf16[1,128,4096]{1,2,0:T(8,128)(2,1)}, u32[]{:S(2)}) copy-start(bf16[1,128,4096]{1,2,0:T(8,128)(2,1)} %copy-done.3) | copy-start | bytes 3145732
  123.2 3.6 %collective-permute-start.4 = (bf16[128,512]{0,1:T(8,128)(2,1)S(1)}, bf16[128,512]{0,1:T(8,128)(2,1)S(1)}, u32[]{:S(2)}, u32[]{:S(2)}) collective-permute-start(bf16[128,512]{0,1:T(8,128)(2,1)S(1)} %get-tuple-element.22), channel_id=1, source_target_pairs={{4,0},{8,4},{12,8},{16,12},{20,16},{24,20},{28,24},{5,1},{9,5},{13... | collective-permute-start | bytes 393224 | tf_op jit(solution)/shard_map/ppermute | solution.py:28
  124.5 21.3 %collective-permute-start.5 = (bf16[128,512]{0,1:T(8,128)(2,1)S(1)}, bf16[128,512]{0,1:T(8,128)(2,1)S(1)}, u32[]{:S(2)}, u32[]{:S(2)}) collective-permute-start(bf16[128,512]{0,1:T(8,128)(2,1)S(1)} %get-tuple-element.23), channel_id=1, source_target_pairs={{8,0},{12,4},{16,8},{20,12},{24,16},{28,20},{9,1},{13,5},{17,9},{2... | collective-permute-start | bytes 393224 | tf_op jit(solution)/shard_map/ppermute | solution.py:28
  (6 other events, 8.2 us)
Sparse Core Ops, SparseCore 0:
  46.4 52.3 reduce-scatter.1
  100.5 86.1 all-gather.2
